TPU v7x, 128 devices: a whole 4x4x4 slice. The times are simulated.
128 devices in a mesh: rows: 4 (over x), cols: 32 (over y, z, core).
Axes of the slice: x: 4, y: 4, z: 4, core: 2. Of those that a mesh axis runs over, the one named last changes fastest.
Arguments:
- weight: bfloat16 [8192, 16384], P('rows', 'cols'), may hold values from -0.046875 to 0.046875
- hess_inv: float32 [16384, 16384], P('rows', 'cols'), as said below
- selected: int32 [3, 64], replicated, may hold values from 0 to 16383, as said below
- block_mask: int32 [8192, 128], P('rows'), may hold values 0 or 1
- row_limits: int32 [8192], P('rows'), may hold values from 16 to 128
- calibration: bfloat16 [1024, 16384], P(None, 'cols'), may hold values from -6 to 6
Outputs:
- pruned: bfloat16 [8192, 16384], P('rows', 'cols')
- layer_error: float32 [8192, 1024], P('rows', 'cols')
Inputs may be any that keep to these rules, and one draw needn't show every extreme that they name: `selected`: all 192 entries differ; 0 and 16383 are among them. `hess_inv`: symmetric positive definite.
All inputs are finite; a program needn't handle non-finite values. No bound on the sum of `block_mask` on one device may be relied on, other than what follows from the above.
Results may differ from a plain program's by a relative error of at most 0.005.
Values may be sent and summed in bfloat16 or wider, within the bound.
A program may use at most 128 MiB of HBM per device.

v0:
```python
import jax
import jax.numpy as jnp
from jax import lax
from jax.sharding import PartitionSpec as P

BLK = 128


def local(weight, hess_inv, selected, block_mask, row_limits, calibration):
    rows_local, cols_local = hess_inv.shape
    out_local = weight.shape[0]
    group = lax.axis_size("cols")
    row_offset = lax.axis_index("rows") * rows_local
    col_offset = lax.axis_index("cols") * cols_local
    chosen = selected.reshape(-1)
    row_place = chosen - row_offset
    row_inside = (row_place >= 0) & (row_place < rows_local)
    own_rows = jnp.where(
        row_inside[:, None], jnp.take(hess_inv, jnp.clip(row_place, 0, rows_local - 1), axis=0), 0.0
    )
    onehot = (
        lax.broadcasted_iota(jnp.int32, (cols_local, chosen.shape[0]), 0)
        == (chosen - col_offset)[None, :]
    )
    square = lax.psum(
        jnp.dot(own_rows, onehot.astype(jnp.float32), precision=lax.Precision.HIGHEST),
        ("rows", "cols"),
    )
    panel = lax.psum(own_rows, "rows")
    weight_cols = lax.psum(
        jnp.dot(weight, onehot.astype(jnp.bfloat16), preferred_element_type=jnp.float32).astype(
            jnp.bfloat16
        ),
        "cols",
    )
    factor = jnp.linalg.cholesky(square)
    coeffs = jax.scipy.linalg.cho_solve((factor, True), panel)
    wide = weight.astype(jnp.float32)
    refit = wide - jnp.dot(weight_cols.astype(jnp.float32), coeffs, precision=lax.Precision.HIGHEST)
    blocks_local = cols_local // BLK
    running_count = jnp.cumsum(block_mask, axis=1)
    retained = block_mask * (running_count <= row_limits[:, None]).astype(jnp.int32)
    own_blocks = lax.dynamic_slice_in_dim(
        retained, lax.axis_index("cols") * blocks_local, blocks_local, 1
    )
    masked = (
        refit.reshape(out_local, blocks_local, BLK) * own_blocks.astype(jnp.float32)[:, :, None]
    ).reshape(out_local, cols_local)
    pruned = masked.astype(jnp.bfloat16)
    difference = (wide - masked).astype(jnp.bfloat16)
    tokens = calibration.shape[0]
    partial = lax.dot_general(
        calibration.reshape(group, tokens // group, cols_local),
        difference,
        (((2,), (1,)), ((), ())),
        preferred_element_type=jnp.float32,
    ).astype(jnp.bfloat16)
    pieces = lax.all_to_all(partial, "cols", split_axis=0, concat_axis=0, tiled=True)
    layer_error = jnp.sum(pieces.astype(jnp.float32), axis=0).T
    return (pruned, layer_error)


def solution(mesh):
    placed = (
        P("rows", "cols"),
        P("rows", "cols"),
        P(),
        P("rows", None),
        P("rows"),
        P(None, "cols"),
    )
    return jax.shard_map(
        local,
        mesh=mesh,
        in_specs=placed,
        out_specs=(P("rows", "cols"), P("rows", "cols")),
        check_vma=False,
    )
```

profile of v0, /device:TPU:1, one launch (start us, length us, event | category | flops | bytes accessed | tf_op | source)
XLA Modules:
  0.0 391.7 jit_solution(5587726836660570919)
XLA Ops:
  7.2 0.8 compare_and_fusion.1
  8.1 0.7 subtract_clamp_fusion
  9.2 5.2 %gather_fusion = f32[192,512]{1,0:T(8,128)} fusion(f32[4096,512]{1,0:T(8,128)} %param.7, s32[1024]{0:T(1024)S(1)} %pad_clamp_fusion), kind=kCustom, calls=%fused_computation | custom fusion | bytes 787200 | tf_op jit(solution)/shard_map/jit(_take)/gather | solution.py:19
  14.3 1.1 select_select_fusion
  15.5 1.3 fusion.5
  16.8 0.7 all-reduce.11.cloned.1.call-update
  17.6 1.8 fusion.2
  20.0 2.5 copy.10
  22.5 3.1 reduce_window_sum.11
  25.6 0.9 fusion.20
  26.5 1.3 copy.12
  27.8 136.7 %all-reduce.9.cloned.1.call-done = f32[192,192]{0,1:T(8,128)} async-done(((f32[192,192]{0,1:T(8,128)}), f32[192,192]{0,1:T(8,128)}) %all-reduce.9.cloned.1.call-update) | async-done | bytes 147472 | tf_op jit(solution)/shard_map/psum | solution.py:25
  164.5 1.0 copy.9
  165.6 1.0 fusion.15
  166.6 11.7 %cholesky.51 = f32[128,128]{1,0:T(8,128)S(1)} custom-call(f32[128,128]{1,0:T(8,128)S(1)} %cholesky.124), custom_call_target="Cholesky" | custom-call | tf_op jit(solution)/shard_map/jit(cholesky)/cholesky | solution.py:36
  178.9 10.4 %custom-call.18 = f32[1,128,128]{1,2,0:T(8,128)} custom-call(f32[1,128,128]{2,1,0:T(8,128)S(1)} %get-tuple-element.23), custom_call_target="InvertDiagBlocksLowerTriangular" | custom-call | tf_op jit(solution)/shard_map/jit(cholesky)/cholesky | solution.py:36
  189.4 0.9 cholesky.119
  190.2 1.0 constant_dynamic-update-slice_fusion
  191.3 0.8 convolution_subtract_fusion.2
  192.1 6.6 %cholesky.110 = f32[64,64]{1,0:T(8,128)S(1)} custom-call(f32[64,64]{1,0:T(8,128)} %convolution_subtract_fusion.2), custom_call_target="Cholesky" | custom-call | tf_op jit(solution)/shard_map/jit(cholesky)/cholesky | solution.py:36
  200.6 0.9 fusion.16
  202.2 20.5 %custom-call.19 = f32[2,128,128]{1,2,0:T(8,128)S(1)} custom-call(f32[2,128,128]{2,1,0:T(8,128)} %pad_maximum_fusion), custom_call_target="InvertDiagBlocksLowerTriangular" | custom-call | tf_op jit(solution)/shard_map/jit(_cho_solve)/triangular_solve | solution.py:37
  222.7 1.4 fusion.11
  224.1 1.2 convolution_subtract_fusion.1
  225.7 1.0 fusion.22
  227.1 1.2 fusion.19
  228.3 87.9 %all-reduce.7.cloned.1.call-done = bf16[2048,192]{0,1:T(8,128)(2,1)} async-done(((bf16[2048,192]{0,1:T(8,128)(2,1)}), bf16[2048,192]{0,1:T(8,128)(2,1)}) %all-reduce.7.cloned.1.call-update) | async-done | bytes 786448 | tf_op jit(solution)/shard_map/psum | solution.py:30
  316.2 5.1 %mul.27 = f32[2048,4,128]{2,1,0:T(4,128)S(1)} broadcast(f32[2048,4]{1,0:T(8,128)} %copy.12), dimensions={0,1} | broadcast | bytes 4227072 | tf_op jit(solution)/shard_map/mul | solution.py:47
  321.3 3.7 fusion.27
  325.0 2.4 convert_bitcast_fusion
  327.4 56.3 %all_to_all.5 = bf16[32,32,2048]{2,1,0:T(8,128)(2,1)S(1)} all-to-all(bf16[32,32,2048]{2,1,0:T(8,128)(2,1)S(1)} %convert_bitcast_fusion), channel_id=1, replica_groups=mesh['rows'=4,'cols'=32] {'cols'}, dimensions={0} | all-to-all | bytes 8388608 | tf_op jit(solution)/shard_map/all_to_all | solution.py:58
  383.7 1.5 convert_reduce_fusion
  (39 shorter events, 4.0 us)
Async XLA Ops:
  7.2 317.8 %copy-start = (bf16[1024,512]{1,0:T(8,128)(2,1)S(1)}, bf16[1024,512]{1,0:T(8,128)(2,1)}, u32[]{:S(2)}) copy-start(bf16[1024,512]{1,0:T(8,128)(2,1)} %param.11) | copy-start | bytes 3145732
  7.2 10.4 %copy-start.1 = (bf16[2048,512]{1,0:T(8,128)(2,1)S(1)}, bf16[2048,512]{1,0:T(8,128)(2,1)}, u32[]{:S(2)}) copy-start(bf16[2048,512]{1,0:T(8,128)(2,1)} %param.6) | copy-start | bytes 6291460
  7.2 157.3 %all-reduce.9.cloned.1.call-start = ((), (), s32[]{:S(2)}) async-start(), calls=%async_computation.2 | async-start | bytes 393216 | tf_op jit(solution)/shard_map/psum | solution.py:25
  15.5 1.4 copy-start.2
  16.8 8.9 %copy-start.6 = (s32[2048]{0:T(1024)S(1)}, s32[2048]{0:T(1024)}, u32[]{:S(2)}) copy-start(s32[2048]{0:T(1024)} %param.10) | copy-start | bytes 24580
  16.8 206.0 %all-reduce.11.cloned.1.call-start = ((), (), s32[]{:S(2)}) async-start(), calls=%async_computation.3 | async-start | bytes 786432 | tf_op jit(solution)/shard_map/psum | solution.py:29
  17.5 298.7 %all-reduce.7.cloned.1.call-start = ((), (), s32[]{:S(2)}) async-start(), calls=%async_computation.1 | async-start | bytes 1572864 | tf_op jit(solution)/shard_map/psum | solution.py:30
  178.3 0.7 copy-start.5
  222.7 2.6 copy-start.4
  316.2 5.1 %copy-start.3 = (bf16[2048,192]{0,1:T(8,128)(2,1)S(1)}, bf16[2048,192]{0,1:T(8,128)(2,1)}, u32[]{:S(2)}) copy-start(bf16[2048,192]{0,1:T(8,128)(2,1)} %all-reduce.7.cloned.1.call-done) | copy-start | bytes 2359300
Sparse Core Ops, SparseCore 0:
  16.9 147.6 all-reduce.8
  166.9 38.7 all-reduce.10
  209.0 107.2 all-reduce.6
where the time goes:
time: 393 us; the launch traced here: 392 us
  waiting for transfers between devices  225 us (57%)
  other arithmetic  61.9 us (16%)
  blocking collectives  56.3 us (14%)
  matrix products  16.5 us (4%)
  local copies, waits for them, and re-layouts  16.4 us (4%)
  between operations  15.2 us (4%)
    psum x1, waiting for transfers between devices, local(): lax.psum(jnp.dot(own_rows, onehot.astype(jnp.float32), precision=lax.Prec...  137 us
    psum x1, waiting for transfers between devices, local(): lax.psum(jnp.dot(weight, onehot.astype(jnp.bfloat16), preferred_element_t...  87.9 us
    all_to_all x1, blocking collectives, local(): lax.all_to_all(partial, 'cols', split_axis=0, concat_axis=0, tiled=True)  56.3 us
    another operation x7, other arithmetic, local(): factor = jnp.linalg.cholesky(square)  30.1 us
    another operation x6, other arithmetic, local(): coeffs = jax.scipy.linalg.cho_solve((factor, True), panel)  22.7 us
  transfers between devices with their start and end apart: 3, of which 2 were waited for; matrix products, arithmetic and copies ran while one was open for 19% of the time, Pallas kernels for 0%

commit v1 on v0

--- a/solution.py
+++ b/solution.py
@@ -4,6 +4,11 @@
 from jax.sharding import PartitionSpec as P
 
 BLK = 128
+
+
+def by_each_axis(x, one, other):
+    half = lax.psum(x, one)
+    return lax.psum(half, other)
 
 
 def local(weight, hess_inv, selected, block_mask, row_limits, calibration):
@@ -22,9 +27,10 @@
         lax.broadcasted_iota(jnp.int32, (cols_local, chosen.shape[0]), 0)
         == (chosen - col_offset)[None, :]
     )
-    square = lax.psum(
+    square = by_each_axis(
         jnp.dot(own_rows, onehot.astype(jnp.float32), precision=lax.Precision.HIGHEST),
-        ("rows", "cols"),
+        "rows",
+        "cols",
     )
     panel = lax.psum(own_rows, "rows")
     weight_cols = lax.psum(

time: 393 us -> 351 us (0.89)
  waiting for transfers between devices: 225 us -> 184 us
    psum x1, waiting for transfers between devices: 0.02 us -> 44.4 us  [local(): panel = lax.psum(own_rows, 'rows')]
    psum x1, waiting for transfers between devices: 87.9 us -> 43.7 us  [local(): lax.psum(jnp.dot(weight, onehot.astype(jnp.bfloat16), preferred_element_t...]
    psum x1, waiting for transfers between devices: 137 us -> 96.1 us  [by_each_axis(): return lax.psum(half, other)]
  transfers between devices with their start and end apart: 3 -> 3, of which waited for: 2 -> 3; matrix products, arithmetic and copies ran while one was open for 19% -> 21% of each run, Pallas kernels for 0% -> 0%
where the time goes in v1:
time: 351 us
  waiting for transfers between devices  184 us (52%)
  other arithmetic  61.9 us (18%)
  blocking collectives  56.3 us (16%)
  matrix products  16.5 us (5%)
  local copies, waits for them, and re-layouts  16.4 us (5%)
  between operations  15.2 us (4%)
    psum x1, waiting for transfers between devices, by_each_axis(): return lax.psum(half, other)  96.1 us
    all_to_all x1, blocking collectives, local(): lax.all_to_all(partial, 'cols', split_axis=0, concat_axis=0, tiled=True)  56.3 us
    psum x1, waiting for transfers between devices, local(): panel = lax.psum(own_rows, 'rows')  44.4 us
    psum x1, waiting for transfers between devices, local(): lax.psum(jnp.dot(weight, onehot.astype(jnp.bfloat16), preferred_element_t...  43.7 us
    another operation x7, other arithmetic, local(): factor = jnp.linalg.cholesky(square)  30.1 us
    another operation x6, other arithmetic, local(): coeffs = jax.scipy.linalg.cho_solve((factor, True), panel)  22.7 us
  transfers between devices with their start and end apart: 3, of which 3 were waited for; matrix products, arithmetic and copies ran while one was open for 21% of the time, Pallas kernels for 0%

profile of v1, /device:TPU:1, one launch (start us, length us, event | category | flops | bytes accessed | tf_op | source)
XLA Modules:
  0.0 350.6 jit_solution(7829292902497390477)
XLA Ops:
  7.2 0.8 compare_and_fusion.1
  8.1 0.7 subtract_clamp_fusion
  9.2 5.2 %gather_fusion = f32[192,512]{1,0:T(8,128)} fusion(f32[4096,512]{1,0:T(8,128)} %param.7, s32[1024]{0:T(1024)S(1)} %pad_clamp_fusion), kind=kCustom, calls=%fused_computation | custom fusion | bytes 787200 | tf_op jit(solution)/shard_map/jit(_take)/gather | solution.py:24
  14.3 1.1 select_select_fusion
  15.5 1.3 fusion.5
  16.8 44.4 %all-reduce.12.cloned.1.call-done = (f32[192,512]{1,0:T(8,128)}, f32[192,192]{0,1:T(8,128)}) async-done(((f32[192,512]{1,0:T(8,128)}, f32[192,192]{0,1:T(8,128)}), (f32[192,512]{1,0:T(8,128)}, f32[192,192]{0,1:T(8,128)})) %all-reduce.12.cloned.1.call-update) | async-done | bytes 540688 | tf_op jit(solution)/shard_map/psum | solution.py:35
  61.3 1.8 fusion.2
  63.7 2.5 copy.10
  66.2 3.1 reduce_window_sum.11
  69.3 0.9 fusion.20
  70.2 1.3 copy.12
  71.6 96.1 %all-reduce.10.cloned.1.call-done = f32[192,192]{0,1:T(8,128)} async-done(((f32[192,192]{0,1:T(8,128)}), f32[192,192]{0,1:T(8,128)}) %all-reduce.10.cloned.1.call-update) | async-done | bytes 147472 | tf_op jit(solution)/shard_map/psum | solution.py:11
  167.6 1.0 copy.9
  168.7 1.0 fusion.15
  169.6 11.7 %cholesky.51 = f32[128,128]{1,0:T(8,128)S(1)} custom-call(f32[128,128]{1,0:T(8,128)S(1)} %cholesky.124), custom_call_target="Cholesky" | custom-call | tf_op jit(solution)/shard_map/jit(cholesky)/cholesky | solution.py:42
  182.1 10.4 %custom-call.18 = f32[1,128,128]{1,2,0:T(8,128)} custom-call(f32[1,128,128]{2,1,0:T(8,128)S(1)} %get-tuple-element.25), custom_call_target="InvertDiagBlocksLowerTriangular" | custom-call | tf_op jit(solution)/shard_map/jit(cholesky)/cholesky | solution.py:42
  192.5 0.9 cholesky.119
  193.3 1.0 constant_dynamic-update-slice_fusion
  194.4 0.8 convolution_subtract_fusion.2
  195.2 6.6 %cholesky.110 = f32[64,64]{1,0:T(8,128)S(1)} custom-call(f32[64,64]{1,0:T(8,128)} %convolution_subtract_fusion.2), custom_call_target="Cholesky" | custom-call | tf_op jit(solution)/shard_map/jit(cholesky)/cholesky | solution.py:42
  203.7 0.9 fusion.16
  205.3 20.5 %custom-call.19 = f32[2,128,128]{1,2,0:T(8,128)S(1)} custom-call(f32[2,128,128]{2,1,0:T(8,128)} %pad_maximum_fusion), custom_call_target="InvertDiagBlocksLowerTriangular" | custom-call | tf_op jit(solution)/shard_map/jit(_cho_solve)/triangular_solve | solution.py:43
  225.8 1.4 fusion.11
  227.2 1.2 convolution_subtract_fusion.1
  228.8 1.0 fusion.22
  230.2 1.2 fusion.19
  231.4 43.7 %all-reduce.8.cloned.1.call-done = bf16[2048,192]{0,1:T(8,128)(2,1)} async-done(((bf16[2048,192]{0,1:T(8,128)(2,1)}), bf16[2048,192]{0,1:T(8,128)(2,1)}) %all-reduce.8.cloned.1.call-update) | async-done | bytes 786448 | tf_op jit(solution)/shard_map/psum | solution.py:36
  275.1 5.1 %mul.27 = f32[2048,4,128]{2,1,0:T(4,128)S(1)} broadcast(f32[2048,4]{1,0:T(8,128)} %copy.12), dimensions={0,1} | broadcast | bytes 4227072 | tf_op jit(solution)/shard_map/mul | solution.py:53
  280.2 3.7 %fusion.27 = (bf16[2048,512]{1,0:T(8,128)(2,1)}, f32[2048,512]{1,0:T(8,128)S(1)}) fusion(f32[256,8,4,128]{3,2,1,0:T(4,128)S(1)} %bitcast.48, bf16[2048,192]{0,1:T(8,128)(2,1)S(1)} %copy-done.3, f32[64,512]{1,0:T(8,128)S(1)} %fusion.22, f32[128,512]{1,0:T(8,128)S(1)} %fusion.19, bf16[2048,512]{1,0:T(8,128)(2,1)S(1)} %copy-done.1), kind=kOutput, calls=%fused_computation.66 | convolution fusion | flops 2420211712 | bytes 13762560 | tf_op jit(solution)/shard_map/dot_general | solution.py:45
  283.9 2.4 convert_bitcast_fusion
  286.3 56.3 %all_to_all.5 = bf16[32,32,2048]{2,1,0:T(8,128)(2,1)S(1)} all-to-all(bf16[32,32,2048]{2,1,0:T(8,128)(2,1)S(1)} %convert_bitcast_fusion), channel_id=1, replica_groups=mesh['rows'=4,'cols'=32] {'cols'}, dimensions={0} | all-to-all | bytes 8388608 | tf_op jit(solution)/shard_map/all_to_all | solution.py:64
  342.6 1.5 convert_reduce_fusion
  (39 shorter events, 4.0 us)
Async XLA Ops:
  7.2 276.7 %copy-start = (bf16[1024,512]{1,0:T(8,128)(2,1)S(1)}, bf16[1024,512]{1,0:T(8,128)(2,1)}, u32[]{:S(2)}) copy-start(bf16[1024,512]{1,0:T(8,128)(2,1)} %param.11) | copy-start | bytes 3145732
  7.2 54.1 %copy-start.1 = (bf16[2048,512]{1,0:T(8,128)(2,1)S(1)}, bf16[2048,512]{1,0:T(8,128)(2,1)}, u32[]{:S(2)}) copy-start(bf16[2048,512]{1,0:T(8,128)(2,1)} %param.6) | copy-start | bytes 6291460
  7.2 54.0 %all-reduce.12.cloned.1.call-start = ((), (), s32[]{:S(2)}) async-start(), calls=%async_computation.3 | async-start | bytes 1179648 | tf_op jit(solution)/shard_map/psum | solution.py:35
  15.5 1.3 copy-start.2
  16.8 52.6 %copy-start.6 = (s32[2048]{0:T(1024)S(1)}, s32[2048]{0:T(1024)}, u32[]{:S(2)}) copy-start(s32[2048]{0:T(1024)} %param.10) | copy-start | bytes 24580
  16.8 150.9 %all-reduce.10.cloned.1.call-start = ((), (), s32[]{:S(2)}) async-start(), calls=%async_computation.2 | async-start | bytes 393216 | tf_op jit(solution)/shard_map/psum | solution.py:11
  61.2 213.9 %all-reduce.8.cloned.1.call-start = ((), (), s32[]{:S(2)}) async-start(), calls=%async_computation.1 | async-start | bytes 1572864 | tf_op jit(solution)/shard_map/psum | solution.py:36
  181.4 0.7 copy-start.5
  225.8 2.6 copy-start.4
  275.1 5.1 %copy-start.3 = (bf16[2048,192]{0,1:T(8,128)(2,1)S(1)}, bf16[2048,192]{0,1:T(8,128)(2,1)}, u32[]{:S(2)}) copy-start(bf16[2048,192]{0,1:T(8,128)(2,1)} %all-reduce.8.cloned.1.call-done) | copy-start | bytes 2359300
Sparse Core Ops, SparseCore 0:
  16.9 44.2 all-reduce.11
  64.5 103.1 all-reduce.9
  170.9 104.1 all-reduce.7
